TPU v7x, 512 devices: a whole 4x8x8 slice. The times are simulated.
512 devices in a mesh: blk: 128 (over z, y, x_lo), rep: 4 (over x_hi, core).
Axes of the slice: x: 4 (x_hi: 2, x_lo: 2; x = x_hi * 2 + x_lo), y: 8, z: 8, core: 2. Of those that a mesh axis runs over, the one named last changes fastest.
Arguments:
- left_emb: float32 [32768, 256], P('blk'), may hold values from -6 to 6
- left_state: float32 [32768], P('blk'), may hold values from 0.3 to 30
- right_emb: float32 [32768, 256], P('blk'), may hold values from -8 to 8
- right_state: float32 [32768], P('blk'), may hold values from 0.3 to 30
- relation: float32 [2, 256, 256], replicated, may hold values from -0.375 to 0.375
- relation_state: float32 [2, 256, 256], replicated, may hold values from 5242.88 to 524288
- edge_src: int32 [128, 4, 2, 2, 512], P('blk', 'rep'), may hold values from 0 to 255
- edge_dst: int32 [128, 4, 2, 2, 512], P('blk', 'rep'), may hold values from 0 to 255
- edge_rel: int32 [128, 4, 2, 2, 512], P('blk', 'rep'), may hold values from 0 to 1
- negatives: int32 [128, 4, 2, 2, 512], P('blk', 'rep'), may hold values from 0 to 255
- batch_counts: int32 [128, 4, 2], P('blk', 'rep'), may hold values from 0 to 2, as said below
Outputs:
- left_new: float32 [32768, 256], P('blk')
- left_state_new: float32 [32768], P('blk')
- right_new: float32 [32768, 256], P('blk')
- right_state_new: float32 [32768], P('blk')
- relation_new: float32 [2, 256, 256], replicated
- relation_state_new: float32 [2, 256, 256], replicated
Inputs may be any that keep to these rules, and one draw needn't show every extreme that they name: `batch_counts`: in each bucket the live edge batches of the 4 devices of one blk index number at most 4; in every draw some bucket has exactly that many, with some device at 2.
All inputs are finite; a program needn't handle non-finite values.
Results may differ from a plain program's by a relative error of at most 0.035.
Values sent between devices are 32-bit elements; how exact they have to be, the bound alone decides.
No kernel may reach another device: no remote copies, remote signals or barrier semaphores. Data moves between devices by JAX's collectives and lax.ppermute only.
A program may use at most 64 MiB of HBM per device.

v0:
```python
import jax
import jax.numpy as jnp
from jax import lax
from jax.sharding import PartitionSpec as P

learn_rate = 0.1


def from_behind(block, axis, distance):
    devices = range(lax.axis_size(axis))
    route = [((i - distance) % len(devices), i) for i in devices]
    return lax.ppermute(block, axis, route)


def batch_terms(query_table, right_bf, src_row, dst_row, rel_row, neg_row, live_flag):
    queries = query_table[rel_row, src_row]
    pos_rows = right_bf[dst_row]
    neg_rows = right_bf[neg_row]
    pos_score = jnp.sum(queries.astype(jnp.float32) * pos_rows.astype(jnp.float32), axis=-1)
    neg_score = lax.dot_general(
        queries, neg_rows, (((1,), (1,)), ((), ())), preferred_element_type=jnp.float32
    )
    row_top = jnp.maximum(jnp.max(neg_score, axis=1), pos_score)
    pos_exp = jnp.exp(pos_score - row_top)
    neg_exp = jnp.exp(neg_score - row_top[:, None])
    row_total = pos_exp + jnp.sum(neg_exp, axis=1)
    pos_weight = (pos_exp / row_total - 1.0) * live_flag
    weights = (neg_exp / row_total[:, None] * live_flag).astype(jnp.bfloat16)
    query_grad = jnp.dot(weights, neg_rows, preferred_element_type=jnp.float32) + pos_weight[
        :, None
    ] * pos_rows.astype(jnp.float32)
    neg_grad = lax.dot_general(
        weights, queries, (((0,), (0,)), ((), ())), preferred_element_type=jnp.float32
    )
    pos_grad = pos_weight[:, None] * queries.astype(jnp.float32)
    return (query_grad, neg_grad, pos_grad)


def bucket_terms(left_rows, right_rows, operator_bf, sources, targets, relations, negs, live_flags):
    left_bf = left_rows.astype(jnp.bfloat16)
    right_bf = right_rows.astype(jnp.bfloat16)
    query_table = jnp.einsum(
        "nd,rkd->rnk", left_bf, operator_bf, preferred_element_type=jnp.float32
    ).astype(jnp.bfloat16)
    nrel, rows, width = query_table.shape

    def step(position, carry):
        table_grad, right_grad = carry
        src_row = lax.dynamic_index_in_dim(sources, position, 0, keepdims=False)
        dst_row = lax.dynamic_index_in_dim(targets, position, 0, keepdims=False)
        rel_row = lax.dynamic_index_in_dim(relations, position, 0, keepdims=False)
        neg_row = lax.dynamic_index_in_dim(negs, position, 0, keepdims=False)
        live_flag = lax.dynamic_index_in_dim(live_flags, position, 0, keepdims=False)
        query_grad, neg_grad, pos_grad = batch_terms(
            query_table, right_bf, src_row, dst_row, rel_row, neg_row, live_flag
        )
        table_grad = table_grad.at[rel_row, src_row].add(query_grad)
        right_grad = right_grad.at[neg_row].add(neg_grad).at[dst_row].add(pos_grad)
        return (table_grad, right_grad)

    start = (jnp.zeros((nrel, rows, width), jnp.float32), jnp.zeros((rows, width), jnp.float32))
    table_grad, right_grad = lax.fori_loop(0, sources.shape[0], step, start)
    table_bf = table_grad.astype(jnp.bfloat16)
    left_grad = jnp.einsum("rnk,rkd->nd", table_bf, operator_bf, preferred_element_type=jnp.float32)
    operator_grad = jnp.einsum("rnk,nd->rkd", table_bf, left_bf, preferred_element_type=jnp.float32)
    return (left_grad, right_grad, operator_grad)


def row_update(embedding, accum, gradient):
    accum_next = accum + jnp.mean(gradient * gradient, axis=-1)
    return (embedding - learn_rate * gradient / jnp.sqrt(accum_next)[:, None], accum_next)


def body(
    left_emb,
    left_state,
    right_emb,
    right_state,
    relation,
    relation_state,
    edge_src,
    edge_dst,
    edge_rel,
    negatives,
    batch_counts,
):
    operator_bf = relation.astype(jnp.bfloat16)
    nbatch = edge_src.shape[3]
    left_rows, left_accum = (left_emb, left_state)
    right_rows, right_accum = (right_emb, right_state)
    operator_total = jnp.zeros(relation.shape, jnp.float32)
    for bucket in range(2):
        sources = edge_src[0, 0, bucket]
        targets = edge_dst[0, 0, bucket]
        relations = edge_rel[0, 0, bucket]
        negs = negatives[0, 0, bucket]
        live_flags = (jnp.arange(nbatch) < batch_counts[0, 0, bucket]).astype(jnp.float32)
        left_grad, right_grad, operator_grad = bucket_terms(
            left_rows, right_rows, operator_bf, sources, targets, relations, negs, live_flags
        )
        operator_total = operator_total + lax.psum(operator_grad, ("blk", "rep"))
        left_sum, right_sum = lax.psum((left_grad, right_grad), "rep")
        left_rows, left_accum = row_update(left_rows, left_accum, left_sum)
        right_rows, right_accum = row_update(right_rows, right_accum, right_sum)
        if bucket == 0:
            left_rows, left_accum = from_behind((left_rows, left_accum), "blk", 1)
    relation_state_new = relation_state + operator_total * operator_total
    relation_new = relation - learn_rate * operator_total / jnp.sqrt(relation_state_new)
    return (left_rows, left_accum, right_rows, right_accum, relation_new, relation_state_new)


def solution(mesh):
    in_specs = (
        P("blk", None),
        P("blk"),
        P("blk", None),
        P("blk"),
        P(),
        P(),
        P("blk", "rep", None, None, None),
        P("blk", "rep", None, None, None),
        P("blk", "rep", None, None, None),
        P("blk", "rep", None, None, None),
        P("blk", "rep", None),
    )
    out_specs = (P("blk", None), P("blk"), P("blk", None), P("blk"), P(), P())
    return jax.shard_map(body, mesh=mesh, in_specs=in_specs, out_specs=out_specs, check_vma=False)
```

profile of v0, /device:TPU:1, one launch (start us, length us, event | category | flops | bytes accessed | tf_op | source)
XLA Modules:
  0.0 608.4 jit_solution(12801148130178979247)
XLA Ops:
  14.1 91.3 %while.34 = (s32[]{:T(128)}, f32[2,256,256]{2,1,0:T(8,128)S(1)}, f32[256,256]{1,0:T(8,128)S(1)}, s32[2,512]{1,0:T(2,128)}, s32[2,512]{1,0:T(2,128)}, /*index=5*/...) while((s32[]{:T(128)}, f32[2,256,256]{2,1,0:T(8,128)S(1)}, ...), condition=%wide.region_7.8_spmd, body=%wide.region_0.7_spmd.sunk | while | flops 406075392 | bytes 12953801 | solution.py:62
  20.7 3.2 gather_fusion
  26.3 26.1 %scatter_fusion = f32[2,256,256]{2,1,0:T(8,128)S(1)} fusion(f32[2,256,256]{2,1,0:T(8,128)S(1)} %get-tuple-element.764, s32[512]{0:T(512)S(1)} %bitcast.154, f32[512,256]{1,0:T(8,128)S(1)} %convolution_add_fusion.5), kind=kCustom, calls=%fused_computation.6.clone.1 | custom fusion | flops 131072 | bytes 1576960 | tf_op jit(solution)/shard_map/while/body/eval_jaxpr/scatter-add | solution.py:57
  52.7 3.4 scatter_fusion.1
  56.1 3.6 scatter_custom_fusion.19
  66.3 3.2 gather_fusion
  71.9 26.1 %scatter_fusion = f32[2,256,256]{2,1,0:T(8,128)S(1)} fusion(f32[2,256,256]{2,1,0:T(8,128)S(1)} %get-tuple-element.764, s32[512]{0:T(512)S(1)} %bitcast.154, f32[512,256]{1,0:T(8,128)S(1)} %convolution_add_fusion.5), kind=kCustom, calls=%fused_computation.6.clone.1 | custom fusion | flops 131072 | bytes 1576960 | tf_op jit(solution)/shard_map/while/body/eval_jaxpr/scatter-add | solution.py:57
  98.3 3.4 scatter_fusion.1
  101.8 3.6 scatter_custom_fusion.19
  108.1 57.2 %all-reduce.10.cloned.1.call-done = (f32[256,256]{1,0:T(8,128)}, f32[256,256]{1,0:T(8,128)}) async-done(((f32[256,256]{1,0:T(8,128)}, f32[256,256]{1,0:T(8,128)}), (f32[256,256]{1,0:T(8,128)}, f32[256,256]{1,0:T(8,128)})) %all-reduce.10.cloned.1.call-update) | async-done | bytes 524304 | tf_op jit(solution)/shard_map/psum | solution.py:102
  167.8 2.5 collective-permute-start
  170.9 11.4 %collective-permute-done = f32[256,256]{1,0:T(8,128)S(1)} collective-permute-done((f32[256,256]{1,0:T(8,128)S(1)}, f32[256,256]{1,0:T(8,128)S(1)}, u32[]{:S(2)}, u32[]{:S(2)}) %collective-permute-start) | collective-permute-done | bytes 262176 | tf_op jit(solution)/shard_map/ppermute | solution.py:12
  182.7 91.3 %while.35 = (s32[]{:T(128)}, f32[2,256,256]{2,1,0:T(8,128)S(1)}, f32[256,256]{1,0:T(8,128)S(1)}, s32[2,512]{1,0:T(2,128)}, s32[2,512]{1,0:T(2,128)}, /*index=5*/...) while((s32[]{:T(128)}, f32[2,256,256]{2,1,0:T(8,128)S(1)}, ...), condition=%wide.region_19.20_spmd, body=%wide.region_12.19_spmd.sunk | while | flops 406075392 | bytes 12921097 | solution.py:62
  189.2 3.2 gather_fusion.3
  194.9 26.1 %scatter_fusion.2 = f32[2,256,256]{2,1,0:T(8,128)S(1)} fusion(f32[2,256,256]{2,1,0:T(8,128)S(1)} %get-tuple-element.797, s32[512]{0:T(512)S(1)} %bitcast.155, f32[512,256]{1,0:T(8,128)S(1)} %convolution_add_fusion.6), kind=kCustom, calls=%fused_computation.9.clone.1 | custom fusion | flops 131072 | bytes 1576960 | tf_op jit(solution)/shard_map/while/body/eval_jaxpr/scatter-add | solution.py:57
  221.3 3.4 scatter_fusion.3
  224.8 3.6 scatter_custom_fusion.23
  234.8 3.2 gather_fusion.3
  240.6 26.1 %scatter_fusion.2 = f32[2,256,256]{2,1,0:T(8,128)S(1)} fusion(f32[2,256,256]{2,1,0:T(8,128)S(1)} %get-tuple-element.797, s32[512]{0:T(512)S(1)} %bitcast.155, f32[512,256]{1,0:T(8,128)S(1)} %convolution_add_fusion.6), kind=kCustom, calls=%fused_computation.9.clone.1 | custom fusion | flops 131072 | bytes 1576960 | tf_op jit(solution)/shard_map/while/body/eval_jaxpr/scatter-add | solution.py:57
  267.0 3.4 scatter_fusion.3
  270.5 3.6 scatter_custom_fusion.23
  274.1 2.2 convolution_add_fusion.2
  280.0 262.9 %all-reduce.6.cloned.1.call-done = f32[2,256,256]{2,1,0:T(8,128)} async-done(((f32[2,256,256]{2,1,0:T(8,128)}), f32[2,256,256]{2,1,0:T(8,128)}) %all-reduce.6.cloned.1.call-update) | async-done | bytes 524304 | tf_op jit(solution)/shard_map/psum | solution.py:101
  545.0 51.2 %all-reduce.8.cloned.1.call-done = (f32[256,256]{1,0:T(8,128)}, f32[256,256]{1,0:T(8,128)}) async-done(((f32[256,256]{1,0:T(8,128)}, f32[256,256]{1,0:T(8,128)}), (f32[256,256]{1,0:T(8,128)}, f32[256,256]{1,0:T(8,128)})) %all-reduce.8.cloned.1.call-update) | async-done | bytes 524304 | tf_op jit(solution)/shard_map/psum | solution.py:102
  (162 shorter events, 61.3 us)
Async XLA Ops:
  7.2 158.1 %all-reduce.10.cloned.1.call-start = ((), (), s32[]{:S(2)}) async-start(), calls=%async_computation.2 | async-start | bytes 1048576 | tf_op jit(solution)/shard_map/psum | solution.py:102
  10.6 1.1 copy-start.2
  14.1 1.2 copy-start.11
  56.1 3.6 copy-start.12
  59.7 1.2 copy-start.11
  101.8 3.6 copy-start.12
  106.3 436.5 %all-reduce.6.cloned.1.call-start = ((), (), s32[]{:S(2)}) async-start(), calls=%async_computation | async-start | bytes 1048576 | tf_op jit(solution)/shard_map/psum | solution.py:101
  165.3 1.1 copy-start.9
  166.4 3.9 copy-start.13
  167.7 2.7 copy-start.21
  167.7 2.7 copy-start.3
  167.7 2.7 copy-start.5
  167.8 14.6 %collective-permute-start = (f32[256,256]{1,0:T(8,128)S(1)}, f32[256,256]{1,0:T(8,128)S(1)}, u32[]{:S(2)}, u32[]{:S(2)}) collective-permute-start(f32[256,256]{1,0:T(8,128)S(1)} %divide_subtract_fusion.3), channel_id=1, source_target_pairs={{508,0},{0,4},{4,8},{8,12},{12,16},{16,20},{20,24},{24,28},{28,32}... | collective-permute-start | bytes 786440 | tf_op jit(solution)/shard_map/ppermute | solution.py:12
  224.8 3.6 copy-start.27
  270.4 3.6 copy-start.27
  274.1 2.2 copy-start
  276.3 319.9 %all-reduce.8.cloned.1.call-start = ((), (), s32[]{:S(2)}) async-start(), calls=%async_computation.1 | async-start | bytes 1048576 | tf_op jit(solution)/shard_map/psum | solution.py:102
  276.4 266.5 %copy-start.10 = (f32[2,256,256]{2,1,0:T(8,128)S(1)}, f32[2,256,256]{2,1,0:T(8,128)}, u32[]{:S(2)}) copy-start(f32[2,256,256]{2,1,0:T(8,128)} %param.20) | copy-start | bytes 1572868
  277.3 265.6 %copy-start.7 = (f32[2,256,256]{2,1,0:T(8,128)S(1)}, f32[2,256,256]{2,1,0:T(8,128)}, u32[]{:S(2)}) copy-start(f32[2,256,256]{2,1,0:T(8,128)} %param.19) | copy-start | bytes 1572868
  278.1 322.5 %collective-permute-start.1 = (f32[256]{0:T(256)S(1)}, f32[256]{0:T(256)S(1)}, u32[]{:S(2)}, u32[]{:S(2)}) collective-permute-start(f32[256]{0:T(256)S(1)} %copy-done.25), channel_id=1, source_target_pairs={{508,0},{0,4},{4,8},{8,12},{12,16},{16,20},{20,24},{24,28},{28,32}... | collective-permute-start | bytes 3080 | tf_op jit(solution)/shard_map/ppermute | solution.py:12
  542.9 55.0 %copy-start.6 = (f32[256,256]{1,0:T(8,128)S(1)}, f32[256,256]{1,0:T(8,128)}, u32[]{:S(2)}) copy-start(f32[256,256]{1,0:T(8,128)} %get-tuple-element.559) | copy-start | bytes 786436
  545.0 52.9 %copy-start.4 = (f32[256,256]{1,0:T(8,128)S(1)}, f32[256,256]{1,0:T(8,128)}, u32[]{:S(2)}) copy-start(f32[256,256]{1,0:T(8,128)} %param.17) | copy-start | bytes 786436
  596.2 1.1 copy-start.22
  598.6 1.8 copy-start.8
  (13 other events, 9.2 us)
Sparse Core Ops, SparseCore 0:
  106.5 58.7 all-reduce.9
  276.4 266.3 all-reduce.5
  546.7 49.4 all-reduce.7
where the time goes:
time: 609 us; the launch traced here: 608 us
  waiting for transfers between devices  383 us (63%)
  other arithmetic  158 us (26%)
  local copies, waits for them, and re-layouts  38.7 us (6%)
  between operations  14.1 us (2%)
  matrix products  9.56 us (2%)
    psum x1, waiting for transfers between devices, body(): operator_total = operator_total + lax.psum(operator_grad, ('blk', 'rep'))  263 us
    psum x2, waiting for transfers between devices, body(): left_sum, right_sum = lax.psum((left_grad, right_grad), 'rep')  108 us
    scatter-add x4, other arithmetic, step(): table_grad = table_grad.at[rel_row, src_row].add(query_grad)  104 us
    scatter-add x8, other arithmetic, step(): right_grad = right_grad.at[neg_row].add(neg_grad).at[dst_row].add(pos_grad)  28.1 us
    gather x4, local copies, waits for them, and re-layouts, batch_terms(): queries = query_table[rel_row, src_row]  12.7 us
  transfers between devices with their start and end apart: 5, of which 4 were waited for; matrix products, arithmetic and copies ran while one was open for 1% of the time, Pallas kernels for 0%

commit v1 on v0

--- a/solution.py
+++ b/solution.py
@@ -4,6 +4,11 @@
 from jax.sharding import PartitionSpec as P
 
 learn_rate = 0.1
+
+
+def axis_by_axis(x, one, other):
+    half = lax.psum(x, one)
+    return lax.psum(half, other)
 
 
 def from_behind(block, axis, distance):
@@ -98,7 +103,7 @@
         left_grad, right_grad, operator_grad = bucket_terms(
             left_rows, right_rows, operator_bf, sources, targets, relations, negs, live_flags
         )
-        operator_total = operator_total + lax.psum(operator_grad, ("blk", "rep"))
+        operator_total = operator_total + axis_by_axis(operator_grad, "blk", "rep")
         left_sum, right_sum = lax.psum((left_grad, right_grad), "rep")
         left_rows, left_accum = row_update(left_rows, left_accum, left_sum)
         right_rows, right_accum = row_update(right_rows, right_accum, right_sum)

time: 609 us -> 1440 us (2.36)
  waiting for transfers between devices: 383 us -> 1210 us
    psum x1, waiting for transfers between devices: 263 us -> 1030 us  [axis_by_axis(): half = lax.psum(x, one)]
    psum x2, waiting for transfers between devices: 108 us -> 166 us  [body(): left_sum, right_sum = lax.psum((left_grad, right_grad), 'rep')]
where the time goes in v1:
time: 1440 us; the launch traced here: 1430 us
  waiting for transfers between devices  1210 us (84%)
  other arithmetic  158 us (11%)
  local copies, waits for them, and re-layouts  38 us (3%)
    psum x1, waiting for transfers between devices, axis_by_axis(): half = lax.psum(x, one)  1030 us
    psum x2, waiting for transfers between devices, body(): left_sum, right_sum = lax.psum((left_grad, right_grad), 'rep')  166 us
    scatter-add x4, other arithmetic, step(): table_grad = table_grad.at[rel_row, src_row].add(query_grad)  104 us
  transfers between devices with their start and end apart: 5, of which 4 were waited for; matrix products, arithmetic and copies ran while one was open for 1% of the time, Pallas kernels for 0%

profile of v1, /device:TPU:1, one launch (start us, length us, event | category | flops | bytes accessed | tf_op | source)
XLA Modules:
  0.0 1434.1 jit_solution(17298234412777871406)
XLA Ops:
  14.1 91.3 %while.34 = (s32[]{:T(128)}, f32[2,256,256]{2,1,0:T(8,128)S(1)}, f32[256,256]{1,0:T(8,128)S(1)}, s32[2,512]{1,0:T(2,128)}, s32[2,512]{1,0:T(2,128)}, /*index=5*/...) while((s32[]{:T(128)}, f32[2,256,256]{2,1,0:T(8,128)S(1)}, ...), condition=%wide.region_7.8_spmd, body=%wide.region_0.7_spmd.sunk | while | flops 406075392 | bytes 12953801 | solution.py:67
  20.7 3.2 gather_fusion
  26.3 26.1 %scatter_fusion = f32[2,256,256]{2,1,0:T(8,128)S(1)} fusion(f32[2,256,256]{2,1,0:T(8,128)S(1)} %get-tuple-element.765, s32[512]{0:T(512)S(1)} %bitcast.154, f32[512,256]{1,0:T(8,128)S(1)} %convolution_add_fusion.5), kind=kCustom, calls=%fused_computation.6.clone.1 | custom fusion | flops 131072 | bytes 1576960 | tf_op jit(solution)/shard_map/while/body/eval_jaxpr/scatter-add | solution.py:62
  52.7 3.4 scatter_fusion.1
  56.1 3.6 scatter_custom_fusion.19
  66.3 3.2 gather_fusion
  71.9 26.1 %scatter_fusion = f32[2,256,256]{2,1,0:T(8,128)S(1)} fusion(f32[2,256,256]{2,1,0:T(8,128)S(1)} %get-tuple-element.765, s32[512]{0:T(512)S(1)} %bitcast.154, f32[512,256]{1,0:T(8,128)S(1)} %convolution_add_fusion.5), kind=kCustom, calls=%fused_computation.6.clone.1 | custom fusion | flops 131072 | bytes 1576960 | tf_op jit(solution)/shard_map/while/body/eval_jaxpr/scatter-add | solution.py:62
  98.3 3.4 scatter_fusion.1
  101.8 3.6 scatter_custom_fusion.19
  108.1 57.2 %all-reduce.10.cloned.1.call-done = (f32[256,256]{1,0:T(8,128)}, f32[256,256]{1,0:T(8,128)}) async-done(((f32[256,256]{1,0:T(8,128)}, f32[256,256]{1,0:T(8,128)}), (f32[256,256]{1,0:T(8,128)}, f32[256,256]{1,0:T(8,128)})) %all-reduce.10.cloned.1.call-update) | async-done | bytes 524304 | tf_op jit(solution)/shard_map/psum | solution.py:107
  167.8 2.5 collective-permute-start
  170.9 11.4 collective-permute-done
  182.7 91.3 %while.35 = (s32[]{:T(128)}, f32[2,256,256]{2,1,0:T(8,128)S(1)}, f32[256,256]{1,0:T(8,128)S(1)}, s32[2,512]{1,0:T(2,128)}, s32[2,512]{1,0:T(2,128)}, /*index=5*/...) while((s32[]{:T(128)}, f32[2,256,256]{2,1,0:T(8,128)S(1)}, ...), condition=%wide.region_19.20_spmd, body=%wide.region_12.19_spmd.sunk | while | flops 406075392 | bytes 12921097 | solution.py:67
  189.2 3.2 gather_fusion.3
  194.9 26.1 %scatter_fusion.2 = f32[2,256,256]{2,1,0:T(8,128)S(1)} fusion(f32[2,256,256]{2,1,0:T(8,128)S(1)} %get-tuple-element.798, s32[512]{0:T(512)S(1)} %bitcast.155, f32[512,256]{1,0:T(8,128)S(1)} %convolution_add_fusion.6), kind=kCustom, calls=%fused_computation.9.clone.1 | custom fusion | flops 131072 | bytes 1576960 | tf_op jit(solution)/shard_map/while/body/eval_jaxpr/scatter-add | solution.py:62
  221.3 3.4 scatter_fusion.3
  224.8 3.6 scatter_custom_fusion.23
  234.8 3.2 gather_fusion.3
  240.6 26.1 %scatter_fusion.2 = f32[2,256,256]{2,1,0:T(8,128)S(1)} fusion(f32[2,256,256]{2,1,0:T(8,128)S(1)} %get-tuple-element.798, s32[512]{0:T(512)S(1)} %bitcast.155, f32[512,256]{1,0:T(8,128)S(1)} %convolution_add_fusion.6), kind=kCustom, calls=%fused_computation.9.clone.1 | custom fusion | flops 131072 | bytes 1576960 | tf_op jit(solution)/shard_map/while/body/eval_jaxpr/scatter-add | solution.py:62
  267.0 3.4 scatter_fusion.3
  270.5 3.6 scatter_custom_fusion.23
  274.1 2.2 convolution_add_fusion.2
  277.3 1031.7 %all-reduce.6.cloned.1.call-done = f32[2,256,256]{2,1,0:T(8,128)} async-done(((f32[2,256,256]{2,1,0:T(8,128)}), f32[2,256,256]{2,1,0:T(8,128)}) %all-reduce.6.cloned.1.call-update) | async-done | bytes 524304 | tf_op jit(solution)/shard_map/psum | solution.py:10
  1311.1 108.5 %all-reduce.8.cloned.1.call-done = (f32[256,256]{1,0:T(8,128)}, f32[256,256]{1,0:T(8,128)}, f32[2,256,256]{2,1,0:T(8,128)}) async-done(((f32[256,256]{1,0:T(8,128)}, f32[256,256]{1,0:T(8,128)}, f32[2,256,256]{2,1,0:T(8,128)}), (f32[256,256]{1,0:T(8,128)}, f32[256,256]{1,0:T(8,128)}, f32[2,256,256]{2,1,0:T(8,128)})) %all-reduce.8.cloned.1.call-update) | async-done | bytes 1048592 | tf_op jit(solution)/shard_map/psum | solution.py:107
  (162 shorter events, 60.7 us)
Async XLA Ops:
  7.2 158.1 %all-reduce.10.cloned.1.call-start = ((), (), s32[]{:S(2)}) async-start(), calls=%async_computation.2 | async-start | bytes 1048576 | tf_op jit(solution)/shard_map/psum | solution.py:107
  10.6 1.1 copy-start.2
  14.1 1.2 copy-start.11
  56.1 3.6 copy-start.12
  59.7 1.2 copy-start.11
  101.8 3.6 copy-start.12
  106.3 1202.7 %all-reduce.6.cloned.1.call-start = ((), (), s32[]{:S(2)}) async-start(), calls=%async_computation | async-start | bytes 1048576 | tf_op jit(solution)/shard_map/psum | solution.py:10
  165.3 1.1 copy-start.9
  166.4 3.9 copy-start.13
  167.7 2.7 copy-start.21
  167.7 2.7 copy-start.3
  167.7 2.7 copy-start.5
  167.8 14.6 %collective-permute-start = (f32[256,256]{1,0:T(8,128)S(1)}, f32[256,256]{1,0:T(8,128)S(1)}, u32[]{:S(2)}, u32[]{:S(2)}) collective-permute-start(f32[256,256]{1,0:T(8,128)S(1)} %divide_subtract_fusion.3), channel_id=1, source_target_pairs={{508,0},{0,4},{4,8},{8,12},{12,16},{16,20},{20,24},{24,28},{28,32}... | collective-permute-start | bytes 786440 | tf_op jit(solution)/shard_map/ppermute | solution.py:17
  224.8 3.6 copy-start.27
  270.4 3.6 copy-start.27
  274.1 2.2 copy-start
  276.3 1143.4 %all-reduce.8.cloned.1.call-start = ((), (), s32[]{:S(2)}) async-start(), calls=%async_computation.1 | async-start | bytes 2097152 | tf_op jit(solution)/shard_map/psum | solution.py:107
  276.4 1032.7 %copy-start.25 = (f32[256]{0:T(256)S(1)}, f32[256]{0:T(256)}, u32[]{:S(2)}) copy-start(f32[256]{0:T(256)} %get-tuple-element.572) | copy-start | bytes 3076
  1309.0 112.3 %copy-start.6 = (f32[256,256]{1,0:T(8,128)S(1)}, f32[256,256]{1,0:T(8,128)}, u32[]{:S(2)}) copy-start(f32[256,256]{1,0:T(8,128)} %get-tuple-element.560) | copy-start | bytes 786436
  1309.0 112.3 %copy-start.4 = (f32[256,256]{1,0:T(8,128)S(1)}, f32[256,256]{1,0:T(8,128)}, u32[]{:S(2)}) copy-start(f32[256,256]{1,0:T(8,128)} %param.17) | copy-start | bytes 786436
  1309.1 117.1 %collective-permute-start.1 = (f32[256]{0:T(256)S(1)}, f32[256]{0:T(256)S(1)}, u32[]{:S(2)}, u32[]{:S(2)}) collective-permute-start(f32[256]{0:T(256)S(1)} %copy-done.25), channel_id=1, source_target_pairs={{508,0},{0,4},{4,8},{8,12},{12,16},{16,20},{20,24},{24,28},{28,32}... | collective-permute-start | bytes 3080 | tf_op jit(solution)/shard_map/ppermute | solution.py:17
  1422.0 1.9 copy-start.7
  1422.0 1.9 copy-start.10
  1423.9 2.2 copy-start.8
  (13 other events, 9.6 us)
Sparse Core Ops, SparseCore 0:
  106.5 58.7 all-reduce.9
  276.4 1032.5 all-reduce.5
  1313.1 106.5 all-reduce.7
